TPU v7x, 512 devices: a whole 4x8x8 slice. The times are simulated.
512 devices in a mesh: row: 16 (over z, y_lo), col: 32 (over y_hi, x, core).
Axes of the slice: x: 4, y: 8 (y_hi: 4, y_lo: 2; y = y_hi * 2 + y_lo), z: 8, core: 2. Of those that a mesh axis runs over, the one named last changes fastest.
Arguments:
- amplitudes: float32 [1024, 20480], P('col', 'row'), may hold values from -6 to 6
- integrals: float32 [20480, 20480], P('row', 'col'), may hold values from -0.0390625 to 0.0390625
- occ_energy: float32 [64], replicated, may hold values from -1.5 to -0.25
- vir_energy: float32 [256], replicated, may hold values from 0.25 to 1.5
- occ_first: int32 [1024], P('row'), may hold values from 0 to 63
- occ_second: int32 [1024], P('row'), may hold values from 0 to 63
- vir_first: int32 [20480], P('col'), may hold values from 0 to 255
- vir_second: int32 [20480], P('col'), may hold values from 0 to 255
Outputs:
- update: float32 [1024, 20480], P('row', 'col')
All inputs are finite; a program needn't handle non-finite values.
Results may differ from a plain program's by a relative error of at most 0.00007.
Values sent between devices are 32-bit elements; how exact they have to be, the bound alone decides.
A program may use at most 64 MiB of HBM per device.

v0:
```python
import jax
import jax.numpy as jnp
from jax import lax
from jax.sharding import PartitionSpec as P


def lookup(table, index):
    positions = jnp.arange(table.shape[0], dtype=jnp.int32)
    picked = jnp.where(index[:, None] == positions[None, :], table[None, :], jnp.float32(0.0))
    return jnp.sum(picked, axis=1)


def per_device(
    amplitudes, integrals, occ_energy, vir_energy, occ_first, occ_second, vir_first, vir_second
):
    partial_rows = jnp.dot(
        lax.all_gather(amplitudes, "col", axis=0, tiled=True),
        integrals,
        preferred_element_type=jnp.float32,
        precision=lax.Precision.HIGHEST,
    )
    ladder = lax.psum_scatter(partial_rows, "row", scatter_dimension=0, tiled=True)
    occ_sum = lookup(occ_energy, occ_first) + lookup(occ_energy, occ_second)
    vir_sum = lookup(vir_energy, vir_first) + lookup(vir_energy, vir_second)
    denom = vir_sum[None, :] - occ_sum[:, None]
    return ladder / denom


def solution(mesh):
    placed = (P("col", "row"), P("row", "col"), P(), P(), P("row"), P("row"), P("col"), P("col"))
    return jax.shard_map(
        per_device, mesh=mesh, in_specs=placed, out_specs=P("row", "col"), check_vma=False
    )
```

profile of v0, /device:TPU:4, one launch (start us, length us, event | category | flops | bytes accessed | tf_op | source)
XLA Modules:
  0.0 190.1 jit_solution(13117659675744692757)
XLA Ops:
  6.5 0.0 copy-start
  6.5 0.0 all-gather.2.cloned.1.call-start
  6.5 0.7 all-gather.2.cloned.1.call-update
  7.3 0.0 copy-start.4
  7.3 0.0 copy-start.5
  7.3 0.0 copy-start.6
  7.3 0.0 copy-start.1
  7.3 0.0 copy-start.2
  7.3 0.0 copy-start.3
  7.3 0.0 reduce-scatter.2.cloned.1.call-start
  7.4 76.8 %all-gather.2.cloned.1.call-done = f32[1024,1280]{1,0:T(8,128)} async-done(((f32[32,1280]{1,0:T(8,128)}), f32[1024,1280]{1,0:T(8,128)}) %all-gather.2.cloned.1.call-update) | async-done | bytes 5242896 | tf_op jit(solution)/shard_map/all_gather | solution.py:17
  84.1 0.0 copy-done
  84.1 15.8 %fusion = f32[1024,640]{1,0:T(8,128)} fusion(f32[1024,1280]{1,0:T(8,128)} %all-gather.2.cloned.1.call-done, f32[1280,640]{1,0:T(8,128)S(1)} %copy-done), kind=kOutput, calls=%fused_computation.9 | convolution fusion | flops 10066329600 | bytes 11141120 | tf_op jit(solution)/shard_map/dot_general | solution.py:16
  99.9 0.0 reduce-scatter.2.cloned.1.call-update
  99.9 0.0 copy-done.4
  99.9 0.0 copy-done.5
  99.9 0.0 copy-done.6
  99.9 0.2 select_reduce_fusion.2
  100.1 0.0 copy-done.1
  100.1 0.0 copy-done.2
  100.2 0.0 copy-done.3
  100.2 0.4 select_reduce_fusion
  100.6 81.0 %reduce-scatter.2.cloned.1.call-done = f32[64,640]{1,0:T(8,128)} async-done(((f32[1024,640]{1,0:T(8,128)}), f32[64,640]{1,0:T(8,128)}) %reduce-scatter.2.cloned.1.call-update) | async-done | bytes 163856 | tf_op jit(solution)/shard_map/reduce_scatter | solution.py:22
  181.6 1.7 subtract_divide_fusion
  (2 shorter events, 0.0 us)
Async XLA Ops:
  6.5 77.6 %copy-start = (f32[1280,640]{1,0:T(8,128)S(1)}, f32[1280,640]{1,0:T(8,128)}, u32[]{:S(2)}) copy-start(f32[1280,640]{1,0:T(8,128)} %param.9) | copy-start | bytes 9830404
  6.5 77.6 %all-gather.2.cloned.1.call-start = ((), (), s32[]{:S(2)}) async-start(), calls=%async_computation.1 | async-start | bytes 5406720 | tf_op jit(solution)/shard_map/all_gather | solution.py:17
  7.3 92.7 %copy-start.4 = (s32[64]{0:T(128)S(1)}, s32[64]{0:T(128)}, u32[]{:S(2)}) copy-start(s32[64]{0:T(128)} %param.13) | copy-start | bytes 772
  7.3 92.7 %copy-start.5 = (f32[64]{0:T(128)S(1)}, f32[64]{0:T(128)}, u32[]{:S(2)}) copy-start(f32[64]{0:T(128)} %param.10) | copy-start | bytes 772
  7.3 92.7 %copy-start.6 = (s32[64]{0:T(128)S(1)}, s32[64]{0:T(128)}, u32[]{:S(2)}) copy-start(s32[64]{0:T(128)} %param.12) | copy-start | bytes 772
  7.3 92.8 %copy-start.1 = (s32[640]{0:T(1024)S(1)}, s32[640]{0:T(1024)}, u32[]{:S(2)}) copy-start(s32[640]{0:T(1024)} %param.15) | copy-start | bytes 7684
  7.3 92.8 %copy-start.2 = (s32[640]{0:T(1024)S(1)}, s32[640]{0:T(1024)}, u32[]{:S(2)}) copy-start(s32[640]{0:T(1024)} %param.14) | copy-start | bytes 7684
  7.3 92.8 %copy-start.3 = (f32[256]{0:T(256)S(1)}, f32[256]{0:T(256)}, u32[]{:S(2)}) copy-start(f32[256]{0:T(256)} %param.11) | copy-start | bytes 3076
  7.3 174.3 %reduce-scatter.2.cloned.1.call-start = ((), (), s32[]{:S(2)}) async-start(), calls=%async_computation.2 | async-start | bytes 2785280 | tf_op jit(solution)/shard_map/reduce_scatter | solution.py:22
Sparse Core Ops, SparseCore 0:
  10.5 73.6 all-gather.1
  100.0 81.5 reduce-scatter.1
where the time goes:
time: 190 us
  waiting for transfers between devices  158 us (83%)
  matrix products  15.8 us (8%)
  between operations  13.5 us (7%)
  other arithmetic  2.3 us (1%)
    reduce_scatter x1, waiting for transfers between devices, per_device(): lax.psum_scatter(partial_rows, 'row', scatter_dimension=0, tiled=True)  81 us
    all_gather x1, waiting for transfers between devices, per_device(): lax.all_gather(amplitudes, 'col', axis=0, tiled=True)  76.8 us
    dot_general x1, matrix products, per_device(): jnp.dot(lax.all_gather(amplitudes, 'col', axis=0, tiled=True), integrals,...  15.8 us
  transfers between devices with their start and end apart: 2, of which 2 were waited for; matrix products, arithmetic and copies ran while one was open for 0% of the time, Pallas kernels for 0%

commit v1 on v0

v1 whole, which is shorter than its diff:
```python
import functools

import jax
import jax.numpy as jnp
from jax import lax
from jax.experimental import pallas as pl
from jax.experimental.pallas import tpu as pltpu
from jax.sharding import PartitionSpec as P

MESH = pl.DeviceIdType.MESH
LAG = 2
ORDER = (
    (0, 0), (0, 1), (0, 3), (0, 2), (1, 0), (3, 0), (1, 1), (1, 3),
    (3, 1), (3, 3), (2, 0), (1, 2), (3, 2), (2, 1), (2, 3), (2, 2),
)
STEPS = len(ORDER)
HOPS = 5


def pick(index, values):
    out = index * 0 + values[0]
    for k, value in enumerate(values):
        if value != values[0]:
            out = jnp.where(index == k, value, out)
    return out


def kernel(
    a_hbm, b_hbm, out_ref,
    a_all, b_f32, b_hi, b_lo, part, from_fwd, from_bwd, from_pair,
    own_sem, b_sem, a_send, c_send, a_recv, c_recv, z_send, fwd_recv, bwd_recv, p_send, p_recv,
):
    row, col = lax.axis_index("row"), lax.axis_index("col")
    z, y_lo = row // 2, row % 2
    core, x, y_hi = col % 2, (col // 2) % 4, col // 8

    def at_col(y_to, x_to, core_to):
        return {"row": row, "col": ((y_to % 4) * 4 + x_to % 4) * 2 + core_to}

    x_next, x_prev = at_col(y_hi, x + 1, core), at_col(y_hi, x + 3, core)
    y_next, y_prev = at_col(y_hi + 1, x, core), at_col(y_hi + 3, x, core)
    other_core = at_col(y_hi, x, 1 - core)
    z_next = {"row": ((z + 1) % 8) * 2 + y_lo, "col": col}
    z_prev = {"row": ((z + 7) % 8) * 2 + y_lo, "col": col}
    y_pair = {"row": z * 2 + 1 - y_lo, "col": col}
    everyone = (x_next, x_prev, y_next, y_prev, other_core, z_next, z_prev, y_pair)

    load_b = pltpu.make_async_copy(b_hbm, b_f32, b_sem)
    load_b.start()

    def block_of(dy, dx):
        return ((y_hi + dy) % 4) * 4 + (x + dx) % 4

    own = block_of(0, 0)
    own_copies = [
        pltpu.make_async_copy(a_hbm.at[pl.ds(16 * half, 16), :], a_all.at[own, core, half], own_sem.at[half])
        for half in range(2)
    ]
    for copy in own_copies:
        copy.start()

    barrier = pltpu.get_barrier_semaphore()
    for device in everyone:
        pl.semaphore_signal(barrier, inc=1, device_id=device, device_id_type=MESH)
    pl.semaphore_wait(barrier, len(everyone))

    sent = []

    def move(dy, dx, half, device, number):
        block = block_of(dy, dx)
        mine = (dy, dx) == (0, 0)
        slot = a_all.at[block, core, half]
        return pltpu.make_async_remote_copy(
            src_ref=a_hbm.at[pl.ds(16 * half, 16), :] if mine else slot,
            dst_ref=slot,
            send_sem=a_send.at[number],
            recv_sem=a_recv.at[block, half],
            device_id=device,
            device_id_type=MESH,
        )

    def send(dy, dx, half, device):
        sent.append((dy, dx, half, device, len(sent)))
        move(*sent[-1]).start()

    def to_core(block, half, src):
        return pltpu.make_async_remote_copy(
            src_ref=src,
            dst_ref=a_all.at[block, core, half],
            send_sem=c_send.at[block, half],
            recv_sem=c_recv.at[block, half],
            device_id=other_core,
            device_id_type=MESH,
        )

    def arrive(dy, dx, half):
        block = block_of(dy, dx)
        slot = a_all.at[block, core, half]
        pltpu.make_async_remote_copy(
            src_ref=slot, dst_ref=slot, send_sem=c_send.at[block, half],
            recv_sem=a_recv.at[block, half], device_id=other_core, device_id_type=MESH,
        ).wait_recv()

    def give(dy, dx, half):
        block = block_of(dy, dx)
        to_core(block, half, a_all.at[block, core, half]).start()

    send(0, 0, 0, x_next)
    send(0, 0, 1, x_prev)
    send(0, 0, 0, y_next)
    send(0, 0, 1, y_prev)
    for half in range(2):
        to_core(own, half, a_hbm.at[pl.ds(16 * half, 16), :]).start()
    send(0, 0, 1, x_next)
    send(0, 0, 0, x_prev)
    send(0, 0, 1, y_next)
    send(0, 0, 0, y_prev)

    def both_x(dy, half):
        send(dy, 0, half, x_next)
        send(dy, 0, half, x_prev)
        give(dy, 0, half)

    def step_own_row():
        arrive(0, 1, 1)
        send(0, 1, 1, x_prev)
        give(0, 1, 1)
        arrive(0, 3, 0)
        send(0, 3, 0, x_next)
        give(0, 3, 0)
        arrive(0, 1, 0)
        give(0, 1, 0)
        arrive(0, 3, 1)
        give(0, 3, 1)

    def step_far_x_own_row():
        arrive(1, 0, 1)
        both_x(1, 1)
        send(1, 0, 1, y_prev)
        arrive(3, 0, 0)
        both_x(3, 0)
        send(3, 0, 0, y_next)
        for half in range(2):
            arrive(0, 2, half)
            give(0, 2, half)

    def step_next_rows():
        arrive(1, 0, 0)
        both_x(1, 0)
        arrive(3, 0, 1)
        both_x(3, 1)

    def step_sides_a():
        arrive(1, 1, 1)
        send(1, 1, 1, x_prev)
        give(1, 1, 1)
        arrive(1, 3, 1)
        give(1, 3, 1)
        arrive(3, 3, 0)
        send(3, 3, 0, x_next)
        give(3, 3, 0)
        arrive(3, 1, 0)
        give(3, 1, 0)
        arrive(1, 1, 0)
        give(1, 1, 0)
        arrive(1, 3, 0)
        send(1, 3, 0, x_next)
        give(1, 3, 0)

    def step_sides_b():
        for half in range(2):
            arrive(2, 0, half)
            both_x(2, half)
        arrive(3, 1, 1)
        send(3, 1, 1, x_prev)
        give(3, 1, 1)
        arrive(3, 3, 1)
        give(3, 3, 1)

    def step_far(dy):
        def go():
            for half in range(2):
                arrive(dy, 2, half)
                give(dy, 2, half)
        return go

    def step_last_row():
        arrive(2, 1, 1)
        send(2, 1, 1, x_prev)
        give(2, 1, 1)
        arrive(2, 3, 0)
        send(2, 3, 0, x_next)
        give(2, 3, 0)
        arrive(2, 1, 0)
        give(2, 1, 0)
        arrive(2, 3, 1)
        give(2, 3, 1)

    before = {
        1: step_own_row, 3: step_far_x_own_row, 4: step_next_rows, 6: step_sides_a, 8: step_sides_b,
        11: step_far(1), 12: step_far(3), 13: step_last_row, 15: step_far(2),
    }

    load_b.wait()

    @pl.loop(0, 10)
    def _(tile):
        rows = pl.ds(pl.multiple_of(tile * 128, 128), 128)
        whole = b_f32[rows, :]
        high = whole.astype(jnp.bfloat16)
        b_hi[rows, :] = high
        b_lo[rows, :] = (whole - high.astype(jnp.float32)).astype(jnp.bfloat16)

    for copy in own_copies:
        copy.wait()

    def place(step):
        dy = pick(step, [d for d, _ in ORDER])
        dx = pick(step, [d for _, d in ORDER])
        return dy, dx, block_of(dy, dx)

    def hop_copy(block, kind, device, into, recv):
        return pltpu.make_async_remote_copy(
            src_ref=part.at[block, kind], dst_ref=into.at[block, kind],
            send_sem=z_send.at[block, kind], recv_sem=recv.at[block, kind],
            device_id=device, device_id_type=MESH,
        )

    def pair_copy(block, kind):
        return pltpu.make_async_remote_copy(
            src_ref=part.at[block, kind], dst_ref=from_pair.at[block, kind],
            send_sem=p_send.at[block, kind], recv_sem=p_recv.at[block, kind],
            device_id=y_pair, device_id_type=MESH,
        )

    def steps_to_go(block, kind):
        z_to = block // 2
        return (z_to - z + 8) % 8 if kind == 0 else (z - z_to + 8) % 8

    def act(step, stage):
        valid = (step >= 0) & (step < STEPS)
        step = jnp.clip(step, 0, STEPS - 1)
        dy, dx, block = place(step)
        pair_first = dy == 2
        home_pair = block % 2 == y_lo

        if stage == 0:
            @pl.when(valid & pair_first & ~home_pair)
            def _():
                for kind in range(2):
                    pair_copy(block, kind).start()

        for kind in range(2):
            togo = steps_to_go(block, kind)
            hop = jnp.where(togo <= 4, 4 - togo, togo - 5)
            mine = valid & jnp.where(pair_first, home_pair & (hop + 1 == stage), hop == stage)
            ahead, behind = (z_next, z_prev) if kind == 0 else (z_prev, z_next)

            @pl.when(mine)
            def _():
                if stage >= 1:
                    @pl.when(pair_first)
                    def _():
                        pair_copy(block, kind).wait_recv()
                        part[block, kind] = part[block, kind] + from_pair[block, kind]

                    @pl.when(togo <= 3)
                    def _():
                        hop_copy(block, kind, ahead, from_fwd, fwd_recv).wait_recv()
                        part[block, kind] = part[block, kind] + from_fwd[block, kind]

                    @pl.when((togo == 0) | (togo >= 6))
                    def _():
                        hop_copy(block, kind, behind, from_bwd, bwd_recv).wait_recv()
                        part[block, kind] = part[block, kind] + from_bwd[block, kind]

                @pl.when((togo >= 1) & (togo <= 4))
                def _():
                    hop_copy(block, kind, ahead, from_fwd, fwd_recv).start()

                @pl.when(togo >= 5)
                def _():
                    hop_copy(block, kind, behind, from_bwd, bwd_recv).start()

                if stage >= 4:
                    @pl.when((togo == 0) & ~pair_first & ~home_pair)
                    def _():
                        pair_copy(block, kind).start()

    def body(step, carry):
        for when, go in before.items():
            pl.when(step == when)(go)

        @pl.when(step < STEPS)
        def _():
            _, _, block = place(jnp.minimum(step, STEPS - 1))
            for half in range(2):
                slot = a_all.at[block, 1 - core, half]
                pltpu.make_async_remote_copy(
                    src_ref=slot, dst_ref=slot, send_sem=c_send.at[block, half],
                    recv_sem=c_recv.at[block, half], device_id=other_core, device_id_type=MESH,
                ).wait_recv()
            whole = a_all[block].reshape(64, 1280)
            high = whole.astype(jnp.bfloat16)
            low = (whole - high.astype(jnp.float32)).astype(jnp.bfloat16)
            dot = functools.partial(jnp.dot, preferred_element_type=jnp.float32)
            total = dot(high, b_lo[...]) + dot(low, b_hi[...]) + dot(high, b_hi[...])
            part[block] = total.reshape(2, 32, 640)

        act(step, 0)
        for stage in range(HOPS, 0, -1):
            act(step - LAG * stage, stage)
        return carry

    lax.fori_loop(0, STEPS + LAG * HOPS, body, 0)

    own_dy = (row // 4 - y_hi + 4) % 4

    @pl.when(own_dy != 2)
    def _():
        for kind in range(2):
            pair_copy(row, kind).wait_recv()
            part[row, kind] = part[row, kind] + from_pair[row, kind]

    out_ref[...] = part[row].reshape(64, 640)

    for one in sent:
        move(*one).wait_send()

    @pl.loop(0, STEPS)
    def _(block):
        pair_first = (block // 4 - y_hi + 4) % 4 == 2
        home_pair = block % 2 == y_lo
        for half in range(2):
            to_core(block, half, a_all.at[block, core, half]).wait_send()
        for kind in range(2):
            togo = steps_to_go(block, kind)

            @pl.when((togo != 0) & (home_pair | ~pair_first))
            def _():
                hop_copy(block, kind, z_next, from_fwd, fwd_recv).wait_send()

            @pl.when(~home_pair & (pair_first | (togo == 0)))
            def _():
                pair_copy(block, kind).wait_send()


def lookup(table, index):
    positions = jnp.arange(table.shape[0], dtype=jnp.int32)
    picked = jnp.where(index[:, None] == positions[None, :], table[None, :], jnp.float32(0.0))
    return jnp.sum(picked, axis=1)


def per_device(
    amplitudes, integrals, occ_energy, vir_energy, occ_first, occ_second, vir_first, vir_second
):
    dma = pltpu.SemaphoreType.DMA
    f32, bf16 = jnp.float32, jnp.bfloat16
    chunk = pltpu.VMEM((16, 2, 32, 640), f32)
    ladder = pl.pallas_call(
        kernel,
        out_shape=jax.ShapeDtypeStruct((64, 640), f32),
        in_specs=[pl.BlockSpec(memory_space=pl.ANY)] * 2,
        out_specs=pl.BlockSpec(memory_space=pltpu.VMEM),
        scratch_shapes=[
            pltpu.VMEM((16, 2, 2, 16, 1280), f32),
            pltpu.VMEM((1280, 640), f32),
            pltpu.VMEM((1280, 640), bf16),
            pltpu.VMEM((1280, 640), bf16),
            chunk, chunk, chunk, chunk,
            dma((2,)), dma, dma((30,)), dma((16, 2)),
            dma((16, 2)), dma((16, 2)),
            dma((16, 2)), dma((16, 2)), dma((16, 2)), dma((16, 2)), dma((16, 2)),
        ],
        compiler_params=pltpu.CompilerParams(
            collective_id=0, has_side_effects=True, vmem_limit_bytes=60 * 1024 * 1024
        ),
    )(amplitudes, integrals)
    occ_sum = lookup(occ_energy, occ_first) + lookup(occ_energy, occ_second)
    vir_sum = lookup(vir_energy, vir_first) + lookup(vir_energy, vir_second)
    denom = vir_sum[None, :] - occ_sum[:, None]
    return ladder / denom


def solution(mesh):
    placed = (P("col", "row"), P("row", "col"), P(), P(), P("row"), P("row"), P("col"), P("col"))
    return jax.shard_map(
        per_device, mesh=mesh, in_specs=placed, out_specs=P("row", "col"), check_vma=False
    )
```

time: 190 us -> 89.8 us (0.47)
  the two profiles are of different devices: /device:TPU:4 before, /device:TPU:104 now
where the time goes in v1:
time: 89.8 us; the launch traced here: 89.7 us
  Pallas kernels  85.9 us (96%)
  other arithmetic  3.71 us (4%)
    pallas_call x1, Pallas kernels, per_device(): pl.pallas_call(kernel, out_shape=jax.ShapeDtypeStruct((64, 640), f32), in...  85.9 us
    reduce_sum x2, other arithmetic, lookup(): return jnp.sum(picked, axis=1)  2.02 us

profile of v1, /device:TPU:104, one launch (start us, length us, event | category | flops | bytes accessed | tf_op | source)
XLA Modules:
  0.0 89.7 jit_solution(15380174115405273907)
XLA Ops:
  0.0 0.9 select_reduce_fusion.2
  0.9 1.2 %select_reduce_fusion = (f32[640]{0:T(1024)S(1)}, f32[640]{0:T(1024)S(1)}) fusion(s32[640]{0:T(1024)} %param.15, f32[256]{0:T(256)} %param.11, s32[640]{0:T(1024)} %param.14), kind=kLoop, calls=%fused_computation | loop fusion | flops 981760 | bytes 11264 | tf_op jit(solution)/shard_map/reduce_sum | solution.py:351
  2.1 85.9 %shard_map.82 = f32[64,640]{1,0:T(8,128)} custom-call(f32[32,1280]{1,0:T(8,128)} %a_hbm.1, f32[1280,640]{1,0:T(8,128)} %b_hbm.1), custom_call_target="tpu_custom_call" | custom-call | tf_op jit(solution)/shard_map/pallas_call | solution.py:360
  88.0 1.7 %subtract_divide_fusion = f32[64,640]{1,0:T(8,128)} fusion(f32[64,640]{1,0:T(8,128)} %shard_map.82, f32[64]{0:T(128)S(1)} %add.15, f32[640]{0:T(1024)S(1)} %add.14), kind=kLoop, calls=%fused_computation.4 | loop fusion | flops 81920 | bytes 330496 | tf_op jit(solution)/shard_map/div | solution.py:382
  (2 shorter events, 0.0 us)

commit v2 on v0

v2 whole, which is shorter than its diff:
```python
import functools

import jax
import jax.numpy as jnp
from jax import lax
from jax.experimental import pallas as pl
from jax.experimental.pallas import tpu as pltpu
from jax.sharding import PartitionSpec as P

MESH = pl.DeviceIdType.MESH
ORDER = (
    (0, 0), (0, 1), (0, 3), (0, 2), (1, 0), (3, 0), (1, 3), (3, 3), (1, 1), (3, 1), (2, 0), (3, 2),
    (1, 2), (2, 3), (2, 1), (2, 2),
)
PAIR_FIRST = ((2, 0), (2, 1), (2, 3), (2, 2),)
AROUND = ((0, 0), (0, 1), (0, 3), (0, 2), (1, 0), (3, 0),)
EVENTS = (
    (),
    ((1, 0, 0), (2, 0, 0), (0, 3, 0), (0, 1, 0), (0, 1, 1), (0, 3, 1), (0, 12, 0), (0, 4, 0), (1, 0, 1), (2,
     0, 1)),
    (),
    ((0, 2, 0), (1, 1, 0), (2, 1, 0), (1, 3, 0), (2, 3, 0), (0, 2, 1), (1, 0, 2), (2, 0, 2), (0, 4, 1), (0,
     12, 1)),
    ((0, 7, 0), (0, 15, 0), (1, 1, 1), (2, 1, 1), (1, 3, 1), (2, 3, 1)),
    (),
    ((1, 2, 0), (2, 2, 0), (0, 5, 0), (0, 13, 0), (1, 0, 3), (2, 0, 3), (2, 4, 0), (1, 12, 0), (2, 12, 0), (1,
     4, 0), (0, 8, 0), (0, 7, 1), (0, 15, 1), (1, 1, 2), (2, 1, 2), (1, 3, 2), (2, 3, 2), (1, 2, 1), (2, 2,
     1), (0, 13, 1), (0, 5, 1), (1, 0, 4), (2, 0, 4), (2, 4, 1), (1, 12, 1)),
    (),
    ((0, 8, 1), (2, 12, 1), (1, 4, 1), (2, 7, 0), (1, 15, 0), (1, 7, 0), (2, 15, 0)),
    (),
    ((0, 9, 0), (0, 6, 0), (0, 14, 0), (1, 13, 0), (2, 5, 0), (1, 5, 0), (2, 13, 0)),
    ((1, 1, 3), (1, 3, 3), (2, 1, 3), (2, 3, 3), (2, 2, 2), (1, 2, 2), (1, 12, 2), (1, 0, 5), (2, 4, 2), (2,
     0, 5), (1, 8, 0), (2, 8, 0), (2, 12, 2), (0, 11, 0), (1, 4, 2), (2, 7, 1), (1, 15, 1), (2, 15, 1), (1, 7,
     1), (0, 14, 1), (0, 6, 1), (2, 5, 1), (1, 13, 1), (0, 11, 1), (1, 1, 4), (2, 1, 4), (1, 5, 1), (2, 13,
     1), (1, 3, 4), (0, 9, 1), (2, 3, 4)),
    (),
    ((1, 8, 1), (1, 12, 3), (2, 4, 3), (2, 0, 6), (1, 0, 6), (2, 6, 0), (1, 6, 0), (1, 14, 0), (2, 14, 0), (2,
     8, 1), (2, 12, 3), (1, 4, 3)),
    ((2, 2, 3), (1, 2, 3)),
    ((2, 15, 2), (1, 7, 2), (0, 10, 0), (2, 7, 2), (1, 15, 2), (1, 11, 0), (2, 11, 0), (1, 9, 0), (2, 9, 0),
     (1, 1, 5), (2, 1, 5), (1, 3, 5), (2, 3, 5), (1, 13, 2), (2, 5, 2), (1, 5, 2), (2, 13, 2), (0, 10, 1), (2,
     0, 7), (1, 0, 7), (1, 8, 2), (2, 4, 4), (1, 12, 4), (2, 6, 1), (2, 8, 2), (1, 14, 1), (1, 2, 4), (2, 2,
     4), (1, 6, 1), (2, 12, 4), (2, 14, 1), (2, 15, 3), (1, 7, 3), (1, 4, 4)),
    ((1, 10, 0), (2, 10, 0), (1, 11, 1), (1, 5, 3), (2, 13, 3), (2, 11, 1), (1, 9, 1), (2, 1, 6), (1, 1, 6),
     (2, 7, 3), (1, 15, 3), (2, 3, 6), (2, 9, 1), (1, 3, 6), (2, 4, 5), (1, 12, 5), (2, 2, 5), (1, 2, 5), (1,
     8, 3), (2, 12, 5), (1, 4, 5), (2, 8, 3), (2, 15, 4), (1, 13, 3), (2, 5, 3), (1, 7, 4), (2, 14, 2), (1, 6,
     2), (1, 10, 1), (2, 6, 2), (1, 14, 2), (2, 10, 1), (1, 11, 2), (2, 11, 2), (1, 5, 4), (2, 13, 4), (2, 1,
     7), (1, 9, 2), (2, 7, 4), (1, 15, 4), (2, 3, 7), (2, 9, 2), (1, 1, 7), (1, 3, 7), (2, 2, 6), (1, 2, 6),
     (1, 8, 4), (2, 12, 6), (1, 13, 4), (2, 5, 4), (1, 4, 6), (2, 8, 4), (1, 12, 6), (2, 4, 6), (1, 10, 2),
     (2, 14, 3), (1, 6, 3), (2, 6, 3), (1, 11, 3), (2, 10, 2), (1, 14, 3), (2, 11, 3), (2, 2, 7), (1, 2, 7),
     (1, 9, 3), (2, 9, 3), (1, 8, 5), (2, 8, 5), (1, 12, 7), (2, 4, 7), (2, 12, 7), (1, 10, 3), (1, 4, 7), (2,
     14, 4), (2, 10, 3), (2, 6, 4), (1, 14, 4), (1, 11, 4), (1, 6, 4), (2, 11, 4), (1, 9, 4), (2, 9, 4), (1,
     11, 5), (1, 10, 4), (2, 10, 4), (2, 11, 5), (1, 9, 5), (2, 9, 5), (1, 10, 5), (2, 10, 5)),
)
PIECE = 16


def pick(index, values):
    out = index * 0 + values[0]
    for k, value in enumerate(values):
        if value != values[0]:
            out = jnp.where(index == k, value, out)
    return out


def column(line):
    n = line.shape[1]
    down = lax.broadcasted_iota(jnp.int32, (n, n), 0)
    along = lax.broadcasted_iota(jnp.int32, (n, n), 1)
    return jnp.sum(jnp.where(down == along, line, jnp.zeros_like(line)), axis=1, keepdims=True)


def lookup(table, index):
    n, m = table.shape[1], index.shape[1]
    at = lax.broadcasted_iota(jnp.int32, (n, m), 0)
    return jnp.sum(jnp.where(at == index, column(table), jnp.float32(0.0)), axis=0, keepdims=True)


def kernel(
    a_hbm, b_hbm, occ_energy, vir_energy, occ_first, occ_second, vir_first, vir_second, out_ref,
    a_all, b_f32, b_hi, b_lo, part, from_fwd, from_bwd, from_pair, denom,
    own_sem, b_sem, a_send, c_send, a_recv, c_recv, z_send, fwd_recv, bwd_recv, p_send, p_recv,
):
    row, col = lax.axis_index("row"), lax.axis_index("col")
    z, y_lo = row // 2, row % 2
    core, x, y_hi = col % 2, (col // 2) % 4, col // 8

    def at_col(y_to, x_to, core_to):
        return {"row": row, "col": ((y_to % 4) * 4 + x_to % 4) * 2 + core_to}

    x_next, x_prev = at_col(y_hi, x + 1, core), at_col(y_hi, x + 3, core)
    y_next, y_prev = at_col(y_hi + 1, x, core), at_col(y_hi + 3, x, core)
    other_core = at_col(y_hi, x, 1 - core)
    z_next = {"row": ((z + 1) % 8) * 2 + y_lo, "col": col}
    z_prev = {"row": ((z + 7) % 8) * 2 + y_lo, "col": col}
    y_pair = {"row": z * 2 + 1 - y_lo, "col": col}
    everyone = (x_next, x_prev, y_next, y_prev, other_core, z_next, z_prev, y_pair)

    load_b = pltpu.make_async_copy(b_hbm, b_f32, b_sem)

    ys = [(y_hi + d) % 4 for d in range(4)]
    xs = [(x + d) % 4 for d in range(4)]

    def block_of(dy, dx):
        return ys[dy] * 4 + xs[dx]

    def in_hbm(half):
        return a_hbm.at[pl.ds(16 * half, 16), :]

    own = block_of(0, 0)
    own_copies = [
        pltpu.make_async_copy(in_hbm(half), a_all.at[own, core, half], own_sem.at[half]) for half in range(2)
    ]

    barrier = pltpu.get_barrier_semaphore()
    for device in everyone:
        pl.semaphore_signal(barrier, inc=1, device_id=device, device_id_type=MESH)
    for copy in own_copies:
        copy.start()
    load_b.start()
    pl.semaphore_wait(barrier, len(everyone))

    sent = []

    def move(dy, dx, half, device, number):
        block = block_of(dy, dx)
        slot = a_all.at[block, core, half]
        return pltpu.make_async_remote_copy(
            src_ref=in_hbm(half) if (dy, dx) == (0, 0) else slot,
            dst_ref=slot,
            send_sem=a_send.at[number],
            recv_sem=a_recv.at[block, half],
            device_id=device,
            device_id_type=MESH,
        )

    def send(dy, dx, half, device):
        sent.append((dy, dx, half, device, len(sent)))
        move(*sent[-1]).start()

    def to_core(block, half, src):
        return pltpu.make_async_remote_copy(
            src_ref=src,
            dst_ref=a_all.at[block, core, half],
            send_sem=c_send.at[block, half],
            recv_sem=c_recv.at[block, half],
            device_id=other_core,
            device_id_type=MESH,
        )

    def arrive(block, half, whose, recv):
        slot = a_all.at[block, whose, half]
        pltpu.make_async_remote_copy(
            src_ref=slot, dst_ref=slot, send_sem=c_send.at[block, half],
            recv_sem=recv.at[block, half], device_id=other_core, device_id_type=MESH,
        ).wait_recv()

    def gather_event(dy, dx, half):
        block = block_of(dy, dx)
        arrive(block, half, core, a_recv)
        if dx == 0:
            if (dy, half) == (1, 1):
                send(dy, dx, half, y_prev)
            if (dy, half) == (3, 0):
                send(dy, dx, half, y_next)
            send(dy, dx, half, x_prev if half else x_next)
            send(dy, dx, half, x_next if half else x_prev)
        if (dx, half) == (1, 1):
            send(dy, dx, half, x_prev)
        if (dx, half) == (3, 0):
            send(dy, dx, half, x_next)
        to_core(block, half, a_all.at[block, core, half]).start()

    def hop_copy(block, piece, device, into, recv):
        return pltpu.make_async_remote_copy(
            src_ref=part.at[block, piece], dst_ref=into.at[block, piece],
            send_sem=z_send.at[block, piece], recv_sem=recv.at[block, piece],
            device_id=device, device_id_type=MESH,
        )

    def pair_copy(block, piece):
        return pltpu.make_async_remote_copy(
            src_ref=part.at[block, piece], dst_ref=from_pair.at[block, piece],
            send_sem=p_send.at[block, piece], recv_sem=p_recv.at[block, piece],
            device_id=y_pair, device_id_type=MESH,
        )

    def steps_to_go(block, parity):
        return (block // 2 - z + 8) % 8 if parity == 0 else (z - block // 2 + 8) % 8

    def reduce_event(dy, dx, parity, stage):
        block = block_of(dy, dx)
        togo = steps_to_go(block, parity)
        home = block % 2 == y_lo
        pair_first, around = (dy, dx) in PAIR_FIRST, (dy, dx) in AROUND
        ahead, behind = (z_next, z_prev) if parity == 0 else (z_prev, z_next)
        hop = stage - 1 if pair_first else stage

        def on_pieces(do):
            for piece in (parity, parity + 2):
                do(piece)

        if hop < 0:
            @pl.when(~home)
            def _():
                on_pieces(lambda piece: pair_copy(block, piece).start())
            return

        def case(left, fwd_in, bwd_in, device, into, recv):
            @pl.when((togo == left) & home if pair_first else togo == left)
            def _():
                def do(piece):
                    total = []
                    if pair_first:
                        pair_copy(block, piece).wait_recv()
                        total.append(from_pair)
                    if fwd_in:
                        hop_copy(block, piece, ahead, from_fwd, fwd_recv).wait_recv()
                        total.append(from_fwd)
                    if bwd_in:
                        hop_copy(block, piece, behind, from_bwd, bwd_recv).wait_recv()
                        total.append(from_bwd)
                    if total:
                        part[block, piece] = sum((t[block, piece] for t in total), part[block, piece])
                    if device is not None:
                        hop_copy(block, piece, device, into, recv).start()

                on_pieces(do)
                if device is None and not pair_first:
                    @pl.when(~home)
                    def _():
                        on_pieces(lambda piece: pair_copy(block, piece).start())

        if around:
            if hop < 7:
                case(7 - hop, hop > 0, False, ahead, from_fwd, fwd_recv)
            else:
                case(0, True, False, None, None, None)
        elif hop < 4:
            case(4 - hop, hop > 0, False, ahead, from_fwd, fwd_recv)
            if hop < 3:
                case(5 + hop, False, hop > 0, behind, from_bwd, bwd_recv)
        else:
            case(0, True, True, None, None, None)

    send(0, 0, 0, x_next)
    send(0, 0, 1, x_prev)
    send(0, 0, 0, y_next)
    send(0, 0, 1, y_prev)
    send(0, 0, 1, x_next)
    send(0, 0, 0, x_prev)
    send(0, 0, 1, y_next)
    send(0, 0, 0, y_prev)
    for half in range(2):
        to_core(own, half, in_hbm(half)).start()

    vir_sum = lookup(vir_energy[...], vir_first[...]) + lookup(vir_energy[...], vir_second[...])
    occ_sum = lookup(occ_energy[...], occ_first[...]) + lookup(occ_energy[...], occ_second[...])
    denom[...] = vir_sum - column(occ_sum)

    load_b.wait()

    @pl.loop(0, 10)
    def _(tile):
        rows = pl.ds(pl.multiple_of(tile * 128, 128), 128)
        whole = b_f32[rows, :]
        high = whole.astype(jnp.bfloat16)
        b_hi[rows, :] = high
        b_lo[rows, :] = (whole - high.astype(jnp.float32)).astype(jnp.bfloat16)

    for copy in own_copies:
        copy.wait()

    def run_events(events):
        for kind, name, detail in events:
            if kind == 0:
                gather_event(name // 4, name % 4, detail)
            else:
                reduce_event(name // 4, name % 4, kind - 1, detail)

    def body(step, carry):
        for k, events in enumerate(EVENTS):
            if events and k < len(ORDER):
                pl.when(step == k)(functools.partial(run_events, events))
        block = block_at(step)
        for half in range(2):
            arrive(block, half, 1 - core, c_recv)
        whole = a_all[block].reshape(64, 1280)
        high = whole.astype(jnp.bfloat16)
        low = (whole - high.astype(jnp.float32)).astype(jnp.bfloat16)
        dot = functools.partial(jnp.dot, preferred_element_type=jnp.float32)
        both = dot(jnp.concatenate([high, low], axis=0), b_hi[...])
        total = dot(high, b_lo[...]) + both[64:] + both[:64]
        part[block] = total.reshape(64 // PIECE, PIECE, 640)
        return carry

    def block_at(step):
        dy, dx = pick(step, [d for d, _ in ORDER]), pick(step, [d for _, d in ORDER])
        return ((y_hi + dy) % 4) * 4 + (x + dx) % 4

    lax.fori_loop(0, len(ORDER), body, 0)
    run_events(EVENTS[len(ORDER)])

    def is_pair_first(block):
        dy, dx = (block // 4 - y_hi + 4) % 4, (block % 4 - x + 4) % 4
        return functools.reduce(lambda a, b: a | b, [(dy == a) & (dx == b) for a, b in PAIR_FIRST])

    whole_sum = part[row].reshape(64, 640)
    out_ref[...] = whole_sum / denom[...]

    @pl.when(~is_pair_first(row))
    def _():
        for piece in range(64 // PIECE):
            pair_copy(row, piece).wait_recv()
        out_ref[...] = (part[row].reshape(64, 640) + from_pair[row].reshape(64, 640)) / denom[...]

    for one in sent:
        move(*one).wait_send()

    @pl.loop(0, 16)
    def _(block):
        pair_first = is_pair_first(block)
        home = block % 2 == y_lo
        for half in range(2):
            to_core(block, half, a_all.at[block, core, half]).wait_send()
        left = steps_to_go(block, 0)

        @pl.when((left != 0) & (home | ~pair_first))
        def _():
            for piece in range(64 // PIECE):
                hop_copy(block, piece, z_next, from_fwd, fwd_recv).wait_send()

        @pl.when(~home & (pair_first | (left == 0)))
        def _():
            for piece in range(64 // PIECE):
                pair_copy(block, piece).wait_send()


def per_device(
    amplitudes, integrals, occ_energy, vir_energy, occ_first, occ_second, vir_first, vir_second
):
    dma = pltpu.SemaphoreType.DMA
    f32, bf16 = jnp.float32, jnp.bfloat16
    pieces = 64 // PIECE
    chunk = pltpu.VMEM((16, pieces, PIECE, 640), f32)
    small = (occ_energy, vir_energy, occ_first, occ_second, vir_first, vir_second)
    return pl.pallas_call(
        kernel,
        out_shape=jax.ShapeDtypeStruct((64, 640), f32),
        in_specs=[pl.BlockSpec(memory_space=pl.ANY)] * 2 + [pl.BlockSpec(memory_space=pltpu.VMEM)] * 6,
        out_specs=pl.BlockSpec(memory_space=pltpu.VMEM),
        scratch_shapes=[
            pltpu.VMEM((16, 2, 2, 16, 1280), f32),
            pltpu.VMEM((1280, 640), f32),
            pltpu.VMEM((1280, 640), bf16),
            pltpu.VMEM((1280, 640), bf16),
            chunk, chunk, chunk, chunk,
            pltpu.VMEM((64, 640), f32),
            dma((2,)), dma, dma((30,)), dma((16, 2)),
            dma((16, 2)), dma((16, 2)),
            dma((16, pieces)), dma((16, pieces)), dma((16, pieces)), dma((16, pieces)), dma((16, pieces)),
        ],
        compiler_params=pltpu.CompilerParams(
            collective_id=0, has_side_effects=True, vmem_limit_bytes=60 * 1024 * 1024
        ),
    )(amplitudes, integrals, *(array.reshape(1, -1) for array in small))


def solution(mesh):
    placed = (P("col", "row"), P("row", "col"), P(), P(), P("row"), P("row"), P("col"), P("col"))
    return jax.shard_map(
        per_device, mesh=mesh, in_specs=placed, out_specs=P("row", "col"), check_vma=False
    )
```

time: 190 us -> 75.7 us (0.40)
  the two profiles are of different devices: /device:TPU:4 before, /device:TPU:40 now
where the time goes in v2:
time: 75.7 us; the launch traced here: 75.4 us
  Pallas kernels  71.3 us (94%)
  local copies, waits for them, and re-layouts  4.11 us (5%)
    pallas_call x1, Pallas kernels, per_device(): pl.pallas_call(kernel, out_shape=jax.ShapeDtypeStruct((64, 640), f32), in...  71.3 us
    reshape x2, local copies, waits for them, and re-layouts, per_device(): array.reshape(1, -1)  2.51 us
    unnamed x1, local copies, waits for them, and re-layouts  1.59 us

profile of v2, /device:TPU:40, one launch (start us, length us, event | category | flops | bytes accessed | tf_op | source)
XLA Modules:
  0.0 75.4 jit_solution(17279162737714738152)
XLA Ops:
  0.0 1.3 %reshape.22.vir_first = s32[1,640]{1,0:T(1,128)} reshape(s32[640]{0:T(1024)} %param.14) | data formatting | bytes 5120 | tf_op jit(solution)/shard_map/reshape | solution.py:367
  1.3 1.2 %reshape.23.vir_second = s32[1,640]{1,0:T(1,128)} reshape(s32[640]{0:T(1024)} %param.15) | data formatting | bytes 5120 | tf_op jit(solution)/shard_map/reshape | solution.py:367
  2.5 71.3 %shard_map.82 = f32[64,640]{1,0:T(8,128)} custom-call(f32[32,1280]{1,0:T(8,128)} %a_hbm.1, f32[1280,640]{1,0:T(8,128)} %b_hbm.1, f32[1,64]{1,0:T(1,128)} %bitcast.5, f32[1,256]{1,0:T(1,128)} %bitcast.4, s32[1,64]{1,0:T(1,128)} %bitcast.6, s32[1,64]{1,0:T(1,128)} %bitcast.7, s32[1,640]{1,0:T(1,128)} %reshape.22.vir_first, s32[1,640]{1,0:T(1,128)} %reshape.23.vir_second), custom_call_target="tpu_custom_call" | custom-call | tf_op jit(solution)/shard_map/pallas_call | solution.py:348
  73.9 1.6 %copy.10 = f32[64,640]{1,0:T(8,128)} copy(f32[64,640]{1,0:T(8,128)} %shard_map.82) | data formatting | bytes 327680

commit v3 on v2

--- a/solution.py
+++ b/solution.py
@@ -9,49 +9,51 @@
 
 MESH = pl.DeviceIdType.MESH
 ORDER = (
-    (0, 0), (0, 1), (0, 3), (0, 2), (1, 0), (3, 0), (1, 3), (3, 3), (1, 1), (3, 1), (2, 0), (3, 2),
-    (1, 2), (2, 3), (2, 1), (2, 2),
+    (0, 0), (0, 1), (0, 3), (0, 2), (1, 0), (3, 0), (2, 0), (3, 3), (1, 1), (1, 3), (3, 1), (2, 3),
+    (2, 1), (1, 2), (3, 2), (2, 2),
 )
 PAIR_FIRST = ((2, 0), (2, 1), (2, 3), (2, 2),)
 AROUND = ((0, 0), (0, 1), (0, 3), (0, 2), (1, 0), (3, 0),)
 EVENTS = (
     (),
-    ((1, 0, 0), (2, 0, 0), (0, 3, 0), (0, 1, 0), (0, 1, 1), (0, 3, 1), (0, 12, 0), (0, 4, 0), (1, 0, 1), (2,
+    ((0, 1, 1), (0, 3, 0), (1, 0, 0), (2, 0, 0), (0, 1, 0), (0, 3, 1), (0, 4, 1), (0, 12, 0), (1, 0, 1), (2,
      0, 1)),
     (),
-    ((0, 2, 0), (1, 1, 0), (2, 1, 0), (1, 3, 0), (2, 3, 0), (0, 2, 1), (1, 0, 2), (2, 0, 2), (0, 4, 1), (0,
-     12, 1)),
-    ((0, 7, 0), (0, 15, 0), (1, 1, 1), (2, 1, 1), (1, 3, 1), (2, 3, 1)),
-    (),
-    ((1, 2, 0), (2, 2, 0), (0, 5, 0), (0, 13, 0), (1, 0, 3), (2, 0, 3), (2, 4, 0), (1, 12, 0), (2, 12, 0), (1,
-     4, 0), (0, 8, 0), (0, 7, 1), (0, 15, 1), (1, 1, 2), (2, 1, 2), (1, 3, 2), (2, 3, 2), (1, 2, 1), (2, 2,
-     1), (0, 13, 1), (0, 5, 1), (1, 0, 4), (2, 0, 4), (2, 4, 1), (1, 12, 1)),
-    (),
-    ((0, 8, 1), (2, 12, 1), (1, 4, 1), (2, 7, 0), (1, 15, 0), (1, 7, 0), (2, 15, 0)),
-    (),
-    ((0, 9, 0), (0, 6, 0), (0, 14, 0), (1, 13, 0), (2, 5, 0), (1, 5, 0), (2, 13, 0)),
-    ((1, 1, 3), (1, 3, 3), (2, 1, 3), (2, 3, 3), (2, 2, 2), (1, 2, 2), (1, 12, 2), (1, 0, 5), (2, 4, 2), (2,
-     0, 5), (1, 8, 0), (2, 8, 0), (2, 12, 2), (0, 11, 0), (1, 4, 2), (2, 7, 1), (1, 15, 1), (2, 15, 1), (1, 7,
-     1), (0, 14, 1), (0, 6, 1), (2, 5, 1), (1, 13, 1), (0, 11, 1), (1, 1, 4), (2, 1, 4), (1, 5, 1), (2, 13,
-     1), (1, 3, 4), (0, 9, 1), (2, 3, 4)),
-    (),
-    ((1, 8, 1), (1, 12, 3), (2, 4, 3), (2, 0, 6), (1, 0, 6), (2, 6, 0), (1, 6, 0), (1, 14, 0), (2, 14, 0), (2,
-     8, 1), (2, 12, 3), (1, 4, 3)),
-    ((2, 2, 3), (1, 2, 3)),
-    ((2, 15, 2), (1, 7, 2), (0, 10, 0), (2, 7, 2), (1, 15, 2), (1, 11, 0), (2, 11, 0), (1, 9, 0), (2, 9, 0),
-     (1, 1, 5), (2, 1, 5), (1, 3, 5), (2, 3, 5), (1, 13, 2), (2, 5, 2), (1, 5, 2), (2, 13, 2), (0, 10, 1), (2,
-     0, 7), (1, 0, 7), (1, 8, 2), (2, 4, 4), (1, 12, 4), (2, 6, 1), (2, 8, 2), (1, 14, 1), (1, 2, 4), (2, 2,
-     4), (1, 6, 1), (2, 12, 4), (2, 14, 1), (2, 15, 3), (1, 7, 3), (1, 4, 4)),
-    ((1, 10, 0), (2, 10, 0), (1, 11, 1), (1, 5, 3), (2, 13, 3), (2, 11, 1), (1, 9, 1), (2, 1, 6), (1, 1, 6),
-     (2, 7, 3), (1, 15, 3), (2, 3, 6), (2, 9, 1), (1, 3, 6), (2, 4, 5), (1, 12, 5), (2, 2, 5), (1, 2, 5), (1,
-     8, 3), (2, 12, 5), (1, 4, 5), (2, 8, 3), (2, 15, 4), (1, 13, 3), (2, 5, 3), (1, 7, 4), (2, 14, 2), (1, 6,
-     2), (1, 10, 1), (2, 6, 2), (1, 14, 2), (2, 10, 1), (1, 11, 2), (2, 11, 2), (1, 5, 4), (2, 13, 4), (2, 1,
-     7), (1, 9, 2), (2, 7, 4), (1, 15, 4), (2, 3, 7), (2, 9, 2), (1, 1, 7), (1, 3, 7), (2, 2, 6), (1, 2, 6),
-     (1, 8, 4), (2, 12, 6), (1, 13, 4), (2, 5, 4), (1, 4, 6), (2, 8, 4), (1, 12, 6), (2, 4, 6), (1, 10, 2),
-     (2, 14, 3), (1, 6, 3), (2, 6, 3), (1, 11, 3), (2, 10, 2), (1, 14, 3), (2, 11, 3), (2, 2, 7), (1, 2, 7),
-     (1, 9, 3), (2, 9, 3), (1, 8, 5), (2, 8, 5), (1, 12, 7), (2, 4, 7), (2, 12, 7), (1, 10, 3), (1, 4, 7), (2,
-     14, 4), (2, 10, 3), (2, 6, 4), (1, 14, 4), (1, 11, 4), (1, 6, 4), (2, 11, 4), (1, 9, 4), (2, 9, 4), (1,
-     11, 5), (1, 10, 4), (2, 10, 4), (2, 11, 5), (1, 9, 5), (2, 9, 5), (1, 10, 5), (2, 10, 5)),
+    ((0, 2, 0), (0, 2, 1), (2, 1, 0), (2, 3, 0), (1, 1, 0), (0, 4, 0), (0, 12, 1), (1, 3, 0), (1, 0, 2), (2,
+     0, 2)),
+    ((1, 2, 0), (0, 5, 1), (0, 7, 1), (2, 2, 0)),
+    (),
+    ((1, 3, 1), (0, 15, 0), (2, 3, 1), (1, 1, 1), (2, 1, 1), (0, 8, 0), (0, 8, 1), (1, 12, 0), (1, 4, 0), (2,
+     4, 0), (2, 12, 0), (0, 13, 0), (2, 2, 1), (1, 0, 3), (1, 2, 1), (0, 7, 0), (0, 15, 1), (0, 5, 0)),
+    ((1, 8, 0), (2, 8, 0), (0, 13, 1), (2, 3, 2), (1, 3, 2), (2, 0, 3), (2, 1, 2), (1, 1, 2), (1, 4, 1), (1,
+     12, 1), (0, 6, 1), (2, 12, 1)),
+    (),
+    (),
+    (),
+    ((1, 5, 0), (2, 7, 0), (2, 4, 1), (2, 5, 0), (1, 15, 0), (2, 0, 4), (1, 0, 4), (2, 2, 2), (1, 7, 0), (1,
+     2, 2), (1, 8, 1), (1, 13, 0), (0, 11, 0), (0, 9, 1), (0, 9, 0), (1, 12, 2), (0, 11, 1), (0, 14, 0), (2,
+     13, 0), (2, 12, 2), (2, 8, 1), (2, 4, 2), (1, 4, 2), (2, 1, 3), (2, 15, 0), (2, 0, 5), (1, 1, 3), (1, 3,
+     3), (2, 3, 3), (1, 0, 5), (1, 5, 1), (0, 6, 0), (0, 14, 1)),
+    (),
+    ((2, 9, 0), (1, 8, 2), (2, 5, 1), (1, 7, 1), (2, 7, 1), (1, 12, 3), (2, 8, 2), (2, 13, 1), (1, 13, 1), (1,
+     9, 0), (2, 11, 0), (1, 2, 3), (0, 10, 1), (2, 2, 3), (0, 10, 0), (1, 11, 0), (2, 12, 3), (2, 4, 3), (2,
+     15, 1)),
+    (),
+    ((1, 3, 4), (1, 1, 4), (1, 0, 6), (2, 3, 4), (2, 1, 4), (1, 15, 1), (1, 4, 3), (2, 0, 6), (2, 5, 2), (1,
+     5, 2), (1, 14, 0), (2, 14, 0), (1, 2, 4), (1, 6, 0), (2, 6, 0), (2, 8, 3)),
+    ((1, 7, 2), (1, 13, 2), (1, 12, 4), (2, 13, 2), (2, 7, 2), (1, 15, 2), (1, 9, 1), (2, 9, 1), (2, 15, 2),
+     (2, 2, 4), (1, 3, 5), (1, 1, 5), (2, 3, 5), (1, 10, 0), (2, 10, 0), (2, 1, 5), (2, 0, 7), (1, 11, 1), (2,
+     12, 4), (2, 4, 4), (2, 11, 1), (1, 5, 3), (1, 4, 4), (2, 6, 1), (1, 14, 1), (1, 6, 1), (2, 14, 1), (2, 5,
+     3), (2, 2, 5), (1, 7, 3), (2, 13, 3), (1, 2, 5), (2, 15, 3), (2, 4, 5), (1, 12, 5), (2, 8, 4), (1, 10,
+     1), (1, 8, 4), (1, 8, 3), (2, 9, 2), (2, 7, 3), (1, 1, 6), (1, 4, 5), (2, 11, 2), (2, 12, 5), (1, 9, 2),
+     (2, 1, 6), (2, 3, 6), (2, 10, 1), (1, 11, 2), (1, 5, 4), (1, 13, 3), (1, 3, 6), (1, 14, 2), (1, 15, 3),
+     (1, 0, 7), (2, 14, 2), (1, 2, 6), (1, 6, 2), (2, 6, 2), (2, 5, 4), (2, 13, 4), (2, 2, 6), (1, 1, 7), (1,
+     7, 4), (2, 1, 7), (2, 8, 5), (1, 12, 6), (2, 12, 6), (1, 14, 3), (1, 10, 2), (1, 3, 7), (1, 8, 5), (2, 3,
+     7), (2, 15, 4), (1, 9, 3), (1, 13, 4), (1, 15, 4), (2, 9, 3), (2, 6, 3), (2, 7, 4), (1, 4, 6), (2, 4, 6),
+     (2, 11, 3), (1, 2, 7), (2, 2, 7), (1, 11, 3), (2, 10, 2), (2, 14, 3), (1, 6, 3), (2, 4, 7), (1, 10, 3),
+     (2, 10, 3), (1, 4, 7), (1, 12, 7), (1, 9, 4), (2, 9, 4), (1, 14, 4), (1, 11, 4), (2, 11, 4), (2, 11, 5),
+     (2, 14, 4), (1, 11, 5), (1, 9, 5), (2, 9, 5), (1, 10, 4), (2, 10, 4), (1, 6, 4), (2, 12, 7), (2, 6, 4),
+     (1, 10, 5), (2, 10, 5)),
 )
 PIECE = 16
 
@@ -78,9 +80,16 @@
 
 
 def kernel(
-    a_hbm, b_hbm, occ_energy, vir_energy, occ_first, occ_second, vir_first, vir_second, out_ref,
+    a_hbm, b_hbm, *refs
+):
+    small_hbm, out_ref, small = refs[:6], refs[6], refs[7:13]
+    body_of(a_hbm, b_hbm, small_hbm, out_ref, small, *refs[13:])
+
+
+def body_of(
+    a_hbm, b_hbm, small_hbm, out_ref, small,
     a_all, b_f32, b_hi, b_lo, part, from_fwd, from_bwd, from_pair, denom,
-    own_sem, b_sem, a_send, c_send, a_recv, c_recv, z_send, fwd_recv, bwd_recv, p_send, p_recv,
+    own_sem, b_sem, small_sem, a_send, c_send, a_recv, c_recv, z_send, fwd_recv, bwd_recv, p_send, p_recv,
 ):
     row, col = lax.axis_index("row"), lax.axis_index("col")
     z, y_lo = row // 2, row % 2
@@ -98,6 +107,10 @@
     everyone = (x_next, x_prev, y_next, y_prev, other_core, z_next, z_prev, y_pair)
 
     load_b = pltpu.make_async_copy(b_hbm, b_f32, b_sem)
+    load_small = [
+        pltpu.make_async_copy(src, dst, small_sem.at[k]) for k, (src, dst) in enumerate(zip(small_hbm, small))
+    ]
+    occ_energy, vir_energy, occ_first, occ_second, vir_first, vir_second = small
 
     ys = [(y_hi + d) % 4 for d in range(4)]
     xs = [(x + d) % 4 for d in range(4)]
@@ -117,6 +130,8 @@
     for device in everyone:
         pl.semaphore_signal(barrier, inc=1, device_id=device, device_id_type=MESH)
     for copy in own_copies:
+        copy.start()
+    for copy in load_small:
         copy.start()
     load_b.start()
     pl.semaphore_wait(barrier, len(everyone))
@@ -255,9 +270,13 @@
     for half in range(2):
         to_core(own, half, in_hbm(half)).start()
 
-    vir_sum = lookup(vir_energy[...], vir_first[...]) + lookup(vir_energy[...], vir_second[...])
-    occ_sum = lookup(occ_energy[...], occ_first[...]) + lookup(occ_energy[...], occ_second[...])
-    denom[...] = vir_sum - column(occ_sum)
+    for copy in load_small:
+        copy.wait()
+    occ_sum = column(lookup(occ_energy[...], occ_first[...]) + lookup(occ_energy[...], occ_second[...]))
+    for part_of_line in range(5):
+        some = pl.ds(part_of_line, 1)
+        vir_sum = lookup(vir_energy[...], vir_first[some, :]) + lookup(vir_energy[...], vir_second[some, :])
+        denom[:, 128 * part_of_line : 128 * part_of_line + 128] = vir_sum - occ_sum
 
     load_b.wait()
 
@@ -344,27 +363,28 @@
     f32, bf16 = jnp.float32, jnp.bfloat16
     pieces = 64 // PIECE
     chunk = pltpu.VMEM((16, pieces, PIECE, 640), f32)
-    small = (occ_energy, vir_energy, occ_first, occ_second, vir_first, vir_second)
+    small = [array.reshape(1, -1) for array in (occ_energy, vir_energy, occ_first, occ_second)]
+    small += [array.reshape(5, 128) for array in (vir_first, vir_second)]
     return pl.pallas_call(
         kernel,
         out_shape=jax.ShapeDtypeStruct((64, 640), f32),
-        in_specs=[pl.BlockSpec(memory_space=pl.ANY)] * 2 + [pl.BlockSpec(memory_space=pltpu.VMEM)] * 6,
+        in_specs=[pl.BlockSpec(memory_space=pltpu.HBM)] * 8,
         out_specs=pl.BlockSpec(memory_space=pltpu.VMEM),
-        scratch_shapes=[
+        scratch_shapes=[pltpu.VMEM(array.shape, array.dtype) for array in small] + [
             pltpu.VMEM((16, 2, 2, 16, 1280), f32),
             pltpu.VMEM((1280, 640), f32),
             pltpu.VMEM((1280, 640), bf16),
             pltpu.VMEM((1280, 640), bf16),
             chunk, chunk, chunk, chunk,
             pltpu.VMEM((64, 640), f32),
-            dma((2,)), dma, dma((30,)), dma((16, 2)),
+            dma((2,)), dma, dma((6,)), dma((30,)), dma((16, 2)),
             dma((16, 2)), dma((16, 2)),
             dma((16, pieces)), dma((16, pieces)), dma((16, pieces)), dma((16, pieces)), dma((16, pieces)),
         ],
         compiler_params=pltpu.CompilerParams(
-            collective_id=0, has_side_effects=True, vmem_limit_bytes=60 * 1024 * 1024
+            collective_id=0, has_side_effects=True, vmem_limit_bytes=57 * 1024 * 1024
         ),
-    )(amplitudes, integrals, *(array.reshape(1, -1) for array in small))
+    )(amplitudes, integrals, *small)
 
 
 def solution(mesh):

time: 75.7 us -> 73 us (0.964)
  the two profiles are of different devices: /device:TPU:40 before, /device:TPU:14 now
where the time goes in v3:
time: 73 us; the launch traced here: 72.9 us
  Pallas kernels  71.3 us (98%)
  local copies, waits for them, and re-layouts  1.59 us (2%)
    pallas_call x1, Pallas kernels, per_device(): pl.pallas_call(kernel, out_shape=jax.ShapeDtypeStruct((64, 640), f32), in...  71.3 us
    unnamed x1, local copies, waits for them, and re-layouts  1.59 us

profile of v3, /device:TPU:14, one launch (start us, length us, event | category | flops | bytes accessed | tf_op | source)
XLA Modules:
  0.0 72.9 jit_solution(1660028342175301259)
XLA Ops:
  0.0 71.3 %shard_map.82 = f32[64,640]{1,0:T(8,128)} custom-call(f32[32,1280]{1,0:T(8,128)} %a_hbm.1, f32[1280,640]{1,0:T(8,128)} %b_hbm.1, f32[1,64]{1,0:T(1,128)} %bitcast.9, f32[1,256]{1,0:T(1,128)} %bitcast.8, s32[1,64]{1,0:T(1,128)} %bitcast.10, s32[1,64]{1,0:T(1,128)} %bitcast.11, s32[5,128]{1,0:T(8,128)} %bitcast.6, s32[5,128]{1,0:T(8,128)} %bitcast.7), custom_call_target="tpu_custom_call" | custom-call | tf_op jit(solution)/shard_map/pallas_call | solution.py:368
  71.3 1.6 %copy.10 = f32[64,640]{1,0:T(8,128)} copy(f32[64,640]{1,0:T(8,128)} %shard_map.82) | data formatting | bytes 327680

commit v4 on v3

--- a/solution.py
+++ b/solution.py
@@ -9,51 +9,45 @@
 
 MESH = pl.DeviceIdType.MESH
 ORDER = (
-    (0, 0), (0, 1), (0, 3), (0, 2), (1, 0), (3, 0), (2, 0), (3, 3), (1, 1), (1, 3), (3, 1), (2, 3),
-    (2, 1), (1, 2), (3, 2), (2, 2),
+    ((0, 0),), ((0, 1), (0, 3),), ((0, 2),), ((1, 0), (3, 0),), ((2, 0),), ((1, 1), (1, 3),), ((3,
+    1), (3, 3),), ((2, 1), (2, 3),), ((1, 2), (3, 2),), ((2, 2),),
 )
 PAIR_FIRST = ((2, 0), (2, 1), (2, 3), (2, 2),)
 AROUND = ((0, 0), (0, 1), (0, 3), (0, 2), (1, 0), (3, 0),)
 EVENTS = (
     (),
-    ((0, 1, 1), (0, 3, 0), (1, 0, 0), (2, 0, 0), (0, 1, 0), (0, 3, 1), (0, 4, 1), (0, 12, 0), (1, 0, 1), (2,
+    ((1, 0, 0), (2, 0, 0), (0, 1, 1), (0, 3, 0), (0, 3, 1), (0, 1, 0), (0, 12, 0), (0, 4, 1), (1, 0, 1), (2,
      0, 1)),
+    ((2, 3, 0), (1, 3, 0), (2, 1, 0), (1, 1, 0), (0, 2, 1), (0, 2, 0), (0, 4, 0), (0, 12, 1)),
+    ((1, 0, 2), (2, 0, 2), (1, 2, 0), (2, 2, 0), (0, 15, 0), (2, 3, 1), (0, 7, 1), (0, 13, 0), (0, 5, 1), (2,
+     1, 1), (1, 1, 1)),
+    ((1, 3, 1), (2, 4, 0), (1, 4, 0), (2, 12, 0), (1, 12, 0), (0, 8, 1), (0, 8, 0), (1, 0, 3), (2, 0, 3), (0,
+     5, 0), (0, 7, 0), (1, 1, 2), (0, 15, 1), (0, 13, 1)),
+    ((2, 1, 2), (2, 3, 2), (1, 3, 2), (2, 4, 1), (1, 8, 0), (2, 8, 0), (1, 4, 1), (1, 2, 1), (2, 2, 1), (1,
+     12, 1)),
     (),
-    ((0, 2, 0), (0, 2, 1), (2, 1, 0), (2, 3, 0), (1, 1, 0), (0, 4, 0), (0, 12, 1), (1, 3, 0), (1, 0, 2), (2,
-     0, 2)),
-    ((1, 2, 0), (0, 5, 1), (0, 7, 1), (2, 2, 0)),
-    (),
-    ((1, 3, 1), (0, 15, 0), (2, 3, 1), (1, 1, 1), (2, 1, 1), (0, 8, 0), (0, 8, 1), (1, 12, 0), (1, 4, 0), (2,
-     4, 0), (2, 12, 0), (0, 13, 0), (2, 2, 1), (1, 0, 3), (1, 2, 1), (0, 7, 0), (0, 15, 1), (0, 5, 0)),
-    ((1, 8, 0), (2, 8, 0), (0, 13, 1), (2, 3, 2), (1, 3, 2), (2, 0, 3), (2, 1, 2), (1, 1, 2), (1, 4, 1), (1,
-     12, 1), (0, 6, 1), (2, 12, 1)),
-    (),
-    (),
-    (),
-    ((1, 5, 0), (2, 7, 0), (2, 4, 1), (2, 5, 0), (1, 15, 0), (2, 0, 4), (1, 0, 4), (2, 2, 2), (1, 7, 0), (1,
-     2, 2), (1, 8, 1), (1, 13, 0), (0, 11, 0), (0, 9, 1), (0, 9, 0), (1, 12, 2), (0, 11, 1), (0, 14, 0), (2,
-     13, 0), (2, 12, 2), (2, 8, 1), (2, 4, 2), (1, 4, 2), (2, 1, 3), (2, 15, 0), (2, 0, 5), (1, 1, 3), (1, 3,
-     3), (2, 3, 3), (1, 0, 5), (1, 5, 1), (0, 6, 0), (0, 14, 1)),
-    (),
-    ((2, 9, 0), (1, 8, 2), (2, 5, 1), (1, 7, 1), (2, 7, 1), (1, 12, 3), (2, 8, 2), (2, 13, 1), (1, 13, 1), (1,
-     9, 0), (2, 11, 0), (1, 2, 3), (0, 10, 1), (2, 2, 3), (0, 10, 0), (1, 11, 0), (2, 12, 3), (2, 4, 3), (2,
-     15, 1)),
-    (),
-    ((1, 3, 4), (1, 1, 4), (1, 0, 6), (2, 3, 4), (2, 1, 4), (1, 15, 1), (1, 4, 3), (2, 0, 6), (2, 5, 2), (1,
-     5, 2), (1, 14, 0), (2, 14, 0), (1, 2, 4), (1, 6, 0), (2, 6, 0), (2, 8, 3)),
-    ((1, 7, 2), (1, 13, 2), (1, 12, 4), (2, 13, 2), (2, 7, 2), (1, 15, 2), (1, 9, 1), (2, 9, 1), (2, 15, 2),
-     (2, 2, 4), (1, 3, 5), (1, 1, 5), (2, 3, 5), (1, 10, 0), (2, 10, 0), (2, 1, 5), (2, 0, 7), (1, 11, 1), (2,
-     12, 4), (2, 4, 4), (2, 11, 1), (1, 5, 3), (1, 4, 4), (2, 6, 1), (1, 14, 1), (1, 6, 1), (2, 14, 1), (2, 5,
-     3), (2, 2, 5), (1, 7, 3), (2, 13, 3), (1, 2, 5), (2, 15, 3), (2, 4, 5), (1, 12, 5), (2, 8, 4), (1, 10,
-     1), (1, 8, 4), (1, 8, 3), (2, 9, 2), (2, 7, 3), (1, 1, 6), (1, 4, 5), (2, 11, 2), (2, 12, 5), (1, 9, 2),
-     (2, 1, 6), (2, 3, 6), (2, 10, 1), (1, 11, 2), (1, 5, 4), (1, 13, 3), (1, 3, 6), (1, 14, 2), (1, 15, 3),
-     (1, 0, 7), (2, 14, 2), (1, 2, 6), (1, 6, 2), (2, 6, 2), (2, 5, 4), (2, 13, 4), (2, 2, 6), (1, 1, 7), (1,
-     7, 4), (2, 1, 7), (2, 8, 5), (1, 12, 6), (2, 12, 6), (1, 14, 3), (1, 10, 2), (1, 3, 7), (1, 8, 5), (2, 3,
-     7), (2, 15, 4), (1, 9, 3), (1, 13, 4), (1, 15, 4), (2, 9, 3), (2, 6, 3), (2, 7, 4), (1, 4, 6), (2, 4, 6),
-     (2, 11, 3), (1, 2, 7), (2, 2, 7), (1, 11, 3), (2, 10, 2), (2, 14, 3), (1, 6, 3), (2, 4, 7), (1, 10, 3),
-     (2, 10, 3), (1, 4, 7), (1, 12, 7), (1, 9, 4), (2, 9, 4), (1, 14, 4), (1, 11, 4), (2, 11, 4), (2, 11, 5),
-     (2, 14, 4), (1, 11, 5), (1, 9, 5), (2, 9, 5), (1, 10, 4), (2, 10, 4), (1, 6, 4), (2, 12, 7), (2, 6, 4),
-     (1, 10, 5), (2, 10, 5)),
+    ((1, 0, 4), (2, 12, 1), (0, 14, 0), (1, 13, 0), (0, 6, 1), (1, 5, 0), (2, 0, 4), (2, 5, 0), (2, 13, 0),
+     (1, 7, 0), (2, 7, 0), (1, 15, 0), (2, 15, 0), (1, 1, 3), (2, 1, 3), (2, 4, 2), (1, 12, 2), (1, 3, 3), (0,
+     11, 0), (0, 9, 0), (0, 9, 1), (0, 11, 1), (1, 8, 1), (1, 0, 5), (1, 4, 2), (2, 3, 3), (2, 12, 2), (2, 0,
+     5), (1, 2, 2), (2, 2, 2), (2, 8, 1), (1, 12, 3), (1, 5, 1), (2, 5, 1), (1, 13, 1), (0, 14, 1), (0, 6, 0),
+     (2, 13, 1)),
+    ((1, 15, 1), (2, 7, 1), (1, 8, 2), (1, 7, 1), (1, 1, 4), (2, 4, 3), (2, 15, 1), (2, 1, 4), (1, 9, 0), (2,
+     9, 0), (1, 3, 4), (1, 4, 3), (1, 11, 0), (2, 11, 0), (1, 0, 6)),
+    ((2, 12, 3), (2, 0, 6), (0, 10, 0), (0, 10, 1), (2, 8, 2), (2, 3, 4), (1, 5, 2), (1, 14, 0), (1, 6, 0),
+     (2, 5, 2), (2, 6, 0), (1, 13, 2), (2, 14, 0), (2, 13, 2), (1, 2, 3), (2, 2, 3), (1, 7, 2), (2, 7, 2), (1,
+     1, 5), (2, 1, 5)),
+    ((2, 4, 4), (1, 15, 2), (1, 12, 4), (2, 15, 2), (1, 9, 1), (1, 10, 1), (1, 3, 5), (1, 8, 3), (1, 10, 0),
+     (2, 10, 0), (1, 4, 4), (2, 10, 1), (2, 9, 1), (2, 12, 4), (1, 0, 7), (2, 0, 7), (2, 3, 5), (2, 8, 3), (2,
+     13, 3), (1, 5, 3), (2, 6, 1), (1, 2, 4), (1, 7, 3), (2, 2, 4), (1, 6, 1), (1, 14, 1), (1, 11, 1), (2, 15,
+     3), (1, 1, 6), (2, 5, 3), (2, 14, 1), (1, 12, 5), (1, 9, 2), (2, 4, 5), (2, 1, 6), (1, 3, 6), (1, 13, 3),
+     (2, 11, 1), (1, 10, 2), (2, 10, 2), (1, 8, 4), (1, 4, 5), (2, 9, 2), (2, 3, 6), (2, 12, 5), (2, 7, 3),
+     (1, 15, 3), (2, 8, 4), (1, 2, 5), (1, 5, 4), (2, 13, 4), (2, 2, 5), (2, 5, 4), (1, 3, 7), (1, 6, 2), (1,
+     14, 2), (2, 14, 2), (2, 6, 2), (1, 1, 7), (2, 15, 4), (1, 11, 2), (1, 9, 3), (2, 1, 7), (1, 10, 3), (1,
+     13, 4), (1, 7, 4), (2, 10, 3), (2, 3, 7), (1, 8, 5), (2, 11, 2), (1, 4, 6), (1, 12, 6), (2, 9, 3), (1,
+     15, 4), (2, 4, 6), (2, 12, 6), (2, 8, 5), (2, 7, 4), (1, 2, 6), (2, 2, 6), (1, 14, 3), (2, 6, 3), (1, 6,
+     3), (1, 11, 3), (2, 14, 3), (1, 10, 4), (1, 9, 4), (2, 11, 3), (2, 10, 4), (2, 4, 7), (2, 9, 4), (1, 4,
+     7), (1, 12, 7), (1, 14, 4), (2, 6, 4), (1, 6, 4), (1, 11, 4), (2, 14, 4), (1, 10, 5), (2, 12, 7), (2, 11,
+     4), (2, 10, 5), (1, 11, 5), (2, 9, 5), (1, 9, 5), (1, 2, 7), (2, 2, 7), (2, 11, 5)),
 )
 PIECE = 16
 
@@ -74,9 +68,9 @@
 
 
 def lookup(table, index):
-    n, m = table.shape[1], index.shape[1]
+    n, m = table.shape[0], index.shape[1]
     at = lax.broadcasted_iota(jnp.int32, (n, m), 0)
-    return jnp.sum(jnp.where(at == index, column(table), jnp.float32(0.0)), axis=0, keepdims=True)
+    return jnp.sum(jnp.where(at == index, table, jnp.float32(0.0)), axis=0, keepdims=True)
 
 
 def kernel(
@@ -88,7 +82,7 @@
 
 def body_of(
     a_hbm, b_hbm, small_hbm, out_ref, small,
-    a_all, b_f32, b_hi, b_lo, part, from_fwd, from_bwd, from_pair, denom,
+    a_all, b_f32, b_hi, b_lo, part, from_fwd, from_bwd, from_pair, denom, result,
     own_sem, b_sem, small_sem, a_send, c_send, a_recv, c_recv, z_send, fwd_recv, bwd_recv, p_send, p_recv,
 ):
     row, col = lax.axis_index("row"), lax.axis_index("col")
@@ -270,14 +264,6 @@
     for half in range(2):
         to_core(own, half, in_hbm(half)).start()
 
-    for copy in load_small:
-        copy.wait()
-    occ_sum = column(lookup(occ_energy[...], occ_first[...]) + lookup(occ_energy[...], occ_second[...]))
-    for part_of_line in range(5):
-        some = pl.ds(part_of_line, 1)
-        vir_sum = lookup(vir_energy[...], vir_first[some, :]) + lookup(vir_energy[...], vir_second[some, :])
-        denom[:, 128 * part_of_line : 128 * part_of_line + 128] = vir_sum - occ_sum
-
     load_b.wait()
 
     @pl.loop(0, 10)
@@ -291,6 +277,17 @@
     for copy in own_copies:
         copy.wait()
 
+    def find_denom():
+        for copy in load_small:
+            copy.wait()
+        table = column(occ_energy[...])
+        occ_sum = column(lookup(table, occ_first[...]) + lookup(table, occ_second[...]))
+        table = column(vir_energy[...])
+        for line in range(5):
+            some = pl.ds(line, 1)
+            vir_sum = lookup(table, vir_first[some, :]) + lookup(table, vir_second[some, :])
+            denom[:, 128 * line : 128 * line + 128] = vir_sum - occ_sum
+
     def run_events(events):
         for kind, name, detail in events:
             if kind == 0:
@@ -302,20 +299,37 @@
         for k, events in enumerate(EVENTS):
             if events and k < len(ORDER):
                 pl.when(step == k)(functools.partial(run_events, events))
-        block = block_at(step)
-        for half in range(2):
-            arrive(block, half, 1 - core, c_recv)
-        whole = a_all[block].reshape(64, 1280)
-        high = whole.astype(jnp.bfloat16)
-        low = (whole - high.astype(jnp.float32)).astype(jnp.bfloat16)
         dot = functools.partial(jnp.dot, preferred_element_type=jnp.float32)
-        both = dot(jnp.concatenate([high, low], axis=0), b_hi[...])
-        total = dot(high, b_lo[...]) + both[64:] + both[:64]
-        part[block] = total.reshape(64 // PIECE, PIECE, 640)
+
+        def multiply(blocks):
+            for block in blocks:
+                for half in range(2):
+                    arrive(block, half, 1 - core, c_recv)
+            whole = jnp.concatenate([a_all[block].reshape(64, 1280) for block in blocks], axis=0)
+            high = whole.astype(jnp.bfloat16)
+            low = (whole - high.astype(jnp.float32)).astype(jnp.bfloat16)
+            both = dot(jnp.concatenate([high, low], axis=0), b_hi[...])
+            rows = 64 * len(blocks)
+            total = dot(high, b_lo[...]) + both[rows:] + both[:rows]
+            for k, block in enumerate(blocks):
+                part[block] = total[64 * k : 64 * k + 64].reshape(64 // PIECE, PIECE, 640)
+
+        two = pick(step, [len(names) - 1 for names in ORDER]) == 1
+        first, second = block_at(step, 0), block_at(step, -1)
+        pl.when(step == 2)(find_denom)
+
+        @pl.when(two)
+        def _():
+            multiply((first, second))
+
+        @pl.when(~two)
+        def _():
+            multiply((first,))
+
         return carry
 
-    def block_at(step):
-        dy, dx = pick(step, [d for d, _ in ORDER]), pick(step, [d for _, d in ORDER])
+    def block_at(step, which):
+        dy, dx = (pick(step, [names[which][axis] for names in ORDER]) for axis in range(2))
         return ((y_hi + dy) % 4) * 4 + (x + dx) % 4
 
     lax.fori_loop(0, len(ORDER), body, 0)
@@ -325,14 +339,16 @@
         dy, dx = (block // 4 - y_hi + 4) % 4, (block % 4 - x + 4) % 4
         return functools.reduce(lambda a, b: a | b, [(dy == a) & (dx == b) for a, b in PAIR_FIRST])
 
-    whole_sum = part[row].reshape(64, 640)
-    out_ref[...] = whole_sum / denom[...]
+    result[...] = part[row].reshape(64, 640) / denom[...]
 
     @pl.when(~is_pair_first(row))
     def _():
         for piece in range(64 // PIECE):
             pair_copy(row, piece).wait_recv()
-        out_ref[...] = (part[row].reshape(64, 640) + from_pair[row].reshape(64, 640)) / denom[...]
+        result[...] = (part[row].reshape(64, 640) + from_pair[row].reshape(64, 640)) / denom[...]
+
+    give_result = pltpu.make_async_copy(result, out_ref, b_sem)
+    give_result.start()
 
     for one in sent:
         move(*one).wait_send()
@@ -354,6 +370,8 @@
         def _():
             for piece in range(64 // PIECE):
                 pair_copy(block, piece).wait_send()
+
+    give_result.wait()
 
 
 def per_device(
@@ -369,13 +387,14 @@
         kernel,
         out_shape=jax.ShapeDtypeStruct((64, 640), f32),
         in_specs=[pl.BlockSpec(memory_space=pltpu.HBM)] * 8,
-        out_specs=pl.BlockSpec(memory_space=pltpu.VMEM),
+        out_specs=pl.BlockSpec(memory_space=pltpu.HBM),
         scratch_shapes=[pltpu.VMEM(array.shape, array.dtype) for array in small] + [
             pltpu.VMEM((16, 2, 2, 16, 1280), f32),
             pltpu.VMEM((1280, 640), f32),
             pltpu.VMEM((1280, 640), bf16),
             pltpu.VMEM((1280, 640), bf16),
             chunk, chunk, chunk, chunk,
+            pltpu.VMEM((64, 640), f32),
             pltpu.VMEM((64, 640), f32),
             dma((2,)), dma, dma((6,)), dma((30,)), dma((16, 2)),
             dma((16, 2)), dma((16, 2)),

time: 73 us -> 71.7 us (0.982)
  Pallas kernels: 71.3 us -> 69.9 us
    pallas_call x1, Pallas kernels: 71.3 us -> 69.9 us  [per_device(): pl.pallas_call(kernel, out_shape=jax.ShapeDtypeStruct((64, 640), f32), in...]
where the time goes in v4:
time: 71.7 us; the launch traced here: 71.5 us
  Pallas kernels  69.9 us (97%)
  local copies, waits for them, and re-layouts  1.59 us (2%)
    pallas_call x1, Pallas kernels, per_device(): pl.pallas_call(kernel, out_shape=jax.ShapeDtypeStruct((64, 640), f32), in...  69.9 us
    unnamed x1, local copies, waits for them, and re-layouts  1.59 us

profile of v4, /device:TPU:14, one launch (start us, length us, event | category | flops | bytes accessed | tf_op | source)
XLA Modules:
  0.0 71.5 jit_solution(1797456122759442941)
XLA Ops:
  0.0 69.9 %shard_map.82 = f32[64,640]{1,0:T(8,128)} custom-call(f32[32,1280]{1,0:T(8,128)} %a_hbm.1, f32[1280,640]{1,0:T(8,128)} %b_hbm.1, f32[1,64]{1,0:T(1,128)} %bitcast.9, f32[1,256]{1,0:T(1,128)} %bitcast.8, s32[1,64]{1,0:T(1,128)} %bitcast.10, s32[1,64]{1,0:T(1,128)} %bitcast.11, s32[5,128]{1,0:T(8,128)} %bitcast.6, s32[5,128]{1,0:T(8,128)} %bitcast.7), custom_call_target="tpu_custom_call" | custom-call | tf_op jit(solution)/shard_map/pallas_call | solution.py:386
  70.0 1.6 %copy.10 = f32[64,640]{1,0:T(8,128)} copy(f32[64,640]{1,0:T(8,128)} %shard_map.82) | data formatting | bytes 327680

commit v5 on v4

--- a/solution.py
+++ b/solution.py
@@ -18,36 +18,34 @@
     (),
     ((1, 0, 0), (2, 0, 0), (0, 1, 1), (0, 3, 0), (0, 3, 1), (0, 1, 0), (0, 12, 0), (0, 4, 1), (1, 0, 1), (2,
      0, 1)),
-    ((2, 3, 0), (1, 3, 0), (2, 1, 0), (1, 1, 0), (0, 2, 1), (0, 2, 0), (0, 4, 0), (0, 12, 1)),
-    ((1, 0, 2), (2, 0, 2), (1, 2, 0), (2, 2, 0), (0, 15, 0), (2, 3, 1), (0, 7, 1), (0, 13, 0), (0, 5, 1), (2,
+    ((2, 3, 0), (1, 3, 0), (0, 2, 1), (0, 2, 0), (2, 1, 0), (1, 1, 0), (0, 4, 0), (0, 12, 1)),
+    ((1, 2, 0), (2, 2, 0), (1, 0, 2), (2, 0, 2), (0, 15, 0), (0, 7, 1), (0, 13, 0), (0, 5, 1), (2, 3, 1), (2,
      1, 1), (1, 1, 1)),
-    ((1, 3, 1), (2, 4, 0), (1, 4, 0), (2, 12, 0), (1, 12, 0), (0, 8, 1), (0, 8, 0), (1, 0, 3), (2, 0, 3), (0,
-     5, 0), (0, 7, 0), (1, 1, 2), (0, 15, 1), (0, 13, 1)),
-    ((2, 1, 2), (2, 3, 2), (1, 3, 2), (2, 4, 1), (1, 8, 0), (2, 8, 0), (1, 4, 1), (1, 2, 1), (2, 2, 1), (1,
+    ((2, 4, 0), (1, 4, 0), (2, 12, 0), (1, 12, 0), (0, 8, 1), (1, 3, 1), (0, 8, 0), (1, 0, 3), (2, 0, 3), (0,
+     5, 0), (0, 7, 0), (0, 15, 1), (0, 13, 1), (1, 1, 2)),
+    ((2, 1, 2), (2, 4, 1), (2, 3, 2), (1, 3, 2), (1, 2, 1), (2, 2, 1), (1, 4, 1), (1, 8, 0), (2, 8, 0), (1,
      12, 1)),
-    (),
-    ((1, 0, 4), (2, 12, 1), (0, 14, 0), (1, 13, 0), (0, 6, 1), (1, 5, 0), (2, 0, 4), (2, 5, 0), (2, 13, 0),
-     (1, 7, 0), (2, 7, 0), (1, 15, 0), (2, 15, 0), (1, 1, 3), (2, 1, 3), (2, 4, 2), (1, 12, 2), (1, 3, 3), (0,
-     11, 0), (0, 9, 0), (0, 9, 1), (0, 11, 1), (1, 8, 1), (1, 0, 5), (1, 4, 2), (2, 3, 3), (2, 12, 2), (2, 0,
-     5), (1, 2, 2), (2, 2, 2), (2, 8, 1), (1, 12, 3), (1, 5, 1), (2, 5, 1), (1, 13, 1), (0, 14, 1), (0, 6, 0),
-     (2, 13, 1)),
-    ((1, 15, 1), (2, 7, 1), (1, 8, 2), (1, 7, 1), (1, 1, 4), (2, 4, 3), (2, 15, 1), (2, 1, 4), (1, 9, 0), (2,
-     9, 0), (1, 3, 4), (1, 4, 3), (1, 11, 0), (2, 11, 0), (1, 0, 6)),
-    ((2, 12, 3), (2, 0, 6), (0, 10, 0), (0, 10, 1), (2, 8, 2), (2, 3, 4), (1, 5, 2), (1, 14, 0), (1, 6, 0),
-     (2, 5, 2), (2, 6, 0), (1, 13, 2), (2, 14, 0), (2, 13, 2), (1, 2, 3), (2, 2, 3), (1, 7, 2), (2, 7, 2), (1,
-     1, 5), (2, 1, 5)),
-    ((2, 4, 4), (1, 15, 2), (1, 12, 4), (2, 15, 2), (1, 9, 1), (1, 10, 1), (1, 3, 5), (1, 8, 3), (1, 10, 0),
-     (2, 10, 0), (1, 4, 4), (2, 10, 1), (2, 9, 1), (2, 12, 4), (1, 0, 7), (2, 0, 7), (2, 3, 5), (2, 8, 3), (2,
-     13, 3), (1, 5, 3), (2, 6, 1), (1, 2, 4), (1, 7, 3), (2, 2, 4), (1, 6, 1), (1, 14, 1), (1, 11, 1), (2, 15,
-     3), (1, 1, 6), (2, 5, 3), (2, 14, 1), (1, 12, 5), (1, 9, 2), (2, 4, 5), (2, 1, 6), (1, 3, 6), (1, 13, 3),
-     (2, 11, 1), (1, 10, 2), (2, 10, 2), (1, 8, 4), (1, 4, 5), (2, 9, 2), (2, 3, 6), (2, 12, 5), (2, 7, 3),
-     (1, 15, 3), (2, 8, 4), (1, 2, 5), (1, 5, 4), (2, 13, 4), (2, 2, 5), (2, 5, 4), (1, 3, 7), (1, 6, 2), (1,
-     14, 2), (2, 14, 2), (2, 6, 2), (1, 1, 7), (2, 15, 4), (1, 11, 2), (1, 9, 3), (2, 1, 7), (1, 10, 3), (1,
-     13, 4), (1, 7, 4), (2, 10, 3), (2, 3, 7), (1, 8, 5), (2, 11, 2), (1, 4, 6), (1, 12, 6), (2, 9, 3), (1,
-     15, 4), (2, 4, 6), (2, 12, 6), (2, 8, 5), (2, 7, 4), (1, 2, 6), (2, 2, 6), (1, 14, 3), (2, 6, 3), (1, 6,
-     3), (1, 11, 3), (2, 14, 3), (1, 10, 4), (1, 9, 4), (2, 11, 3), (2, 10, 4), (2, 4, 7), (2, 9, 4), (1, 4,
-     7), (1, 12, 7), (1, 14, 4), (2, 6, 4), (1, 6, 4), (1, 11, 4), (2, 14, 4), (1, 10, 5), (2, 12, 7), (2, 11,
-     4), (2, 10, 5), (1, 11, 5), (2, 9, 5), (1, 9, 5), (1, 2, 7), (2, 2, 7), (2, 11, 5)),
+    ((0, 14, 0), (2, 12, 1), (0, 6, 1)),
+    ((1, 0, 4), (1, 13, 0), (1, 5, 0), (2, 0, 4), (2, 5, 0), (2, 13, 0), (1, 7, 0), (2, 7, 0), (1, 15, 0), (2,
+     15, 0), (1, 1, 3), (2, 1, 3), (2, 4, 2), (0, 11, 0), (0, 9, 0), (0, 9, 1), (0, 11, 1), (1, 12, 2), (1, 3,
+     3), (1, 8, 1), (1, 2, 2), (2, 2, 2), (1, 4, 2), (1, 0, 5), (2, 3, 3), (2, 12, 2), (2, 0, 5), (2, 8, 1),
+     (1, 12, 3), (1, 5, 1), (2, 5, 1), (0, 14, 1), (0, 6, 0), (1, 13, 1), (2, 13, 1), (1, 15, 1)),
+    ((2, 7, 1), (2, 4, 3), (1, 8, 2), (1, 7, 1), (2, 15, 1), (1, 1, 4), (2, 1, 4), (1, 9, 0), (2, 9, 0), (1,
+     3, 4), (1, 4, 3), (1, 11, 0), (2, 11, 0), (1, 0, 6), (0, 10, 0), (0, 10, 1)),
+    ((2, 12, 3), (2, 0, 6), (2, 8, 2), (2, 3, 4), (1, 2, 3), (1, 5, 2), (1, 14, 0), (1, 6, 0), (2, 2, 3), (2,
+     13, 2), (2, 6, 0), (2, 14, 0), (2, 5, 2), (1, 13, 2), (2, 1, 5), (1, 8, 3), (1, 7, 2), (2, 7, 2)),
+    ((2, 4, 4), (1, 12, 4), (1, 15, 2), (1, 1, 5), (2, 15, 2), (1, 9, 1), (2, 8, 3), (1, 10, 1), (1, 3, 5),
+     (1, 4, 4), (2, 10, 1), (1, 10, 0), (2, 9, 1), (2, 10, 0), (2, 12, 4), (1, 0, 7), (2, 0, 7), (2, 3, 5),
+     (1, 2, 4), (2, 13, 3), (2, 2, 4), (2, 6, 1), (1, 5, 3), (1, 14, 1), (1, 6, 1), (1, 7, 3), (1, 11, 1), (1,
+     8, 4), (2, 14, 1), (1, 1, 6), (2, 15, 3), (2, 5, 3), (2, 4, 5), (2, 11, 1), (1, 12, 5), (1, 9, 2), (2, 1,
+     6), (1, 13, 3), (1, 3, 6), (1, 10, 2), (1, 4, 5), (1, 2, 5), (2, 8, 4), (2, 10, 2), (2, 9, 2), (2, 3, 6),
+     (2, 12, 5), (2, 7, 3), (1, 15, 3), (1, 5, 4), (2, 2, 5), (2, 13, 4), (1, 14, 2), (1, 6, 2), (2, 14, 2),
+     (2, 6, 2), (1, 8, 5), (1, 1, 7), (2, 15, 4), (1, 11, 2), (1, 9, 3), (1, 3, 7), (2, 1, 7), (1, 13, 4), (1,
+     7, 4), (2, 8, 5), (1, 10, 3), (2, 11, 2), (1, 4, 6), (2, 10, 3), (1, 12, 6), (2, 9, 3), (2, 4, 6), (1,
+     15, 4), (2, 12, 6), (2, 6, 3), (2, 3, 7), (1, 2, 6), (1, 6, 3), (2, 2, 6), (2, 7, 4), (1, 14, 3), (2, 5,
+     4), (2, 14, 3), (1, 11, 3), (1, 10, 4), (1, 9, 4), (2, 11, 3), (2, 10, 4), (2, 6, 4), (2, 4, 7), (1, 6,
+     4), (1, 4, 7), (2, 9, 4), (1, 14, 4), (1, 12, 7), (2, 14, 4), (1, 11, 4), (2, 12, 7), (1, 10, 5), (2, 11,
+     4), (2, 10, 5), (2, 9, 5), (1, 9, 5), (1, 2, 7), (1, 11, 5), (2, 2, 7), (2, 11, 5)),
 )
 PIECE = 16
 

time: 71.7 us -> 71.4 us (level)
  no operation moved by 1% of the time
where the time goes in v5:
time: 71.4 us; the launch traced here: 71.1 us
  Pallas kernels  69.5 us (97%)
  local copies, waits for them, and re-layouts  1.59 us (2%)
    pallas_call x1, Pallas kernels, per_device(): pl.pallas_call(kernel, out_shape=jax.ShapeDtypeStruct((64, 640), f32), in...  69.5 us
    unnamed x1, local copies, waits for them, and re-layouts  1.59 us

profile of v5, /device:TPU:14, one launch (start us, length us, event | category | flops | bytes accessed | tf_op | source)
XLA Modules:
  0.0 71.1 jit_solution(9077490309211752492)
XLA Ops:
  0.0 69.5 %shard_map.82 = f32[64,640]{1,0:T(8,128)} custom-call(f32[32,1280]{1,0:T(8,128)} %a_hbm.1, f32[1280,640]{1,0:T(8,128)} %b_hbm.1, f32[1,64]{1,0:T(1,128)} %bitcast.9, f32[1,256]{1,0:T(1,128)} %bitcast.8, s32[1,64]{1,0:T(1,128)} %bitcast.10, s32[1,64]{1,0:T(1,128)} %bitcast.11, s32[5,128]{1,0:T(8,128)} %bitcast.6, s32[5,128]{1,0:T(8,128)} %bitcast.7), custom_call_target="tpu_custom_call" | custom-call | tf_op jit(solution)/shard_map/pallas_call | solution.py:384
  69.5 1.6 %copy.10 = f32[64,640]{1,0:T(8,128)} copy(f32[64,640]{1,0:T(8,128)} %shard_map.82) | data formatting | bytes 327680
